TPU v7x, 32 devices: a whole 2x2x4 slice. The times are simulated.
32 devices in a mesh: seq: 8 (over y, x, core), head: 4 (over z).
Axes of the slice: x: 2, y: 2, z: 4, core: 2. Of those that a mesh axis runs over, the one named last changes fastest.
Arguments:
- queries: bfloat16 [1024, 8192], P('seq', 'head'), may hold values from -6 to 6
- keys: bfloat16 [1024, 1024], P('seq'), may hold values from -6 to 6
- values: bfloat16 [1024, 1024], P('seq'), may hold values from -6 to 6
- doc_lengths: int32 [12], replicated, may hold values from 1 to 512, 1024 in all
- fq_weight: bfloat16 [64, 128, 128], P('head'), may hold values from -1 to 1
- fk_weight: bfloat16 [64, 128, 128], P('head'), may hold values from -1 to 1
Outputs:
- residual: float32 [1024, 8192], P('seq', 'head')
- token_loss: float32 [1024], P('seq')
Inputs may be any that keep to these rules, and one draw needn't show every extreme that they name: `doc_lengths`: the 12 documents are packed in order and their lengths sum to 1024; the longest has exactly 512 tokens.
All inputs are finite; a program needn't handle non-finite values.
Results may differ from a plain program's by a relative error of at most 0.0035.
Values may be sent and summed in bfloat16 or wider, within the bound.
A program may use at most 64 MiB of HBM per device.

v0:
```python
import jax
import jax.numpy as jnp
from jax import lax
from jax.sharding import PartitionSpec as P

QH = 64
KVH = 8


NEG = -1e30


def passed_along(block, axis, distance):
    devices = range(lax.axis_size(axis))
    route = [(i - distance, i) for i in devices if i - distance in devices]
    return lax.ppermute(block, axis, route)


def entering(array, axis, join, neutral):
    place = lax.axis_index(axis)
    gathered = jax.tree.map(
        lambda a, kind: lax.all_gather(a.astype(kind), axis),
        array,
        (jnp.bfloat16, jnp.bfloat16, jnp.bfloat16),
    )
    state = jax.tree.map(lambda a, e: jnp.zeros_like(a) + jnp.asarray(e, a.dtype), array, neutral)

    def one(turn, state):
        return join(
            state,
            jax.tree.map(
                lambda a, own: lax.dynamic_index_in_dim(a, turn, 0, False).astype(own.dtype),
                gathered,
                array,
            ),
        )

    return lax.fori_loop(0, place, one, state)


def doc_index(positions, starts):
    return jnp.sum((starts[None, :] <= positions[:, None]).astype(jnp.int32), axis=1) - 1


def feature_map(projected):
    return jnp.concatenate(
        [jax.nn.softmax(projected, axis=-1), jax.nn.softmax(-projected, axis=-1)], axis=-1
    ).astype(jnp.bfloat16)


def chain(earlier, later):
    return (
        earlier[0] * later[0],
        later[1] + later[0] * earlier[1],
        later[2] + later[0] * earlier[2],
    )


def body(queries, keys, values, doc_lengths, fq_weight, fk_weight):
    tok_rows = queries.shape[0]
    heads = fq_weight.shape[0]
    head_dim = fq_weight.shape[1]
    group = QH // KVH
    kv_local = max(1, heads // group)
    repeat = heads // kv_local
    kv_first = lax.axis_index("head") * heads // group
    k_own = lax.dynamic_slice_in_dim(keys, kv_first * head_dim, kv_local * head_dim, 1)
    v_own = lax.dynamic_slice_in_dim(values, kv_first * head_dim, kv_local * head_dim, 1)
    starts = jnp.cumsum(doc_lengths) - doc_lengths
    anchor = lax.axis_index("seq") * tok_rows
    q_pos = anchor + jnp.arange(tok_rows, dtype=jnp.int32)
    q_doc = doc_index(q_pos, starts)
    query_groups = queries.reshape(tok_rows, kv_local, repeat, head_dim)
    first_start = jnp.max(jnp.where(starts <= anchor, starts, 0))
    last_pos = anchor + tok_rows - 1
    scale = head_dim ** (-0.5)

    def attend(carry, pieces, start):
        rows = pieces[0].shape[0]
        needed = (start <= last_pos) & (start + rows - 1 >= first_start)

        def compute(state):
            peak, total, accum = state
            key_segment = pieces[0].reshape(rows, kv_local, head_dim)
            v_piece = pieces[1].reshape(rows, kv_local, head_dim)
            k_pos = start + jnp.arange(rows, dtype=jnp.int32)
            k_doc = doc_index(k_pos, starts)
            mask = (
                (q_doc[:, None] == k_doc[None, :])
                & (k_pos[None, :] <= q_pos[:, None])
                & (k_pos[None, :] >= 0)
            )
            scores = jnp.where(
                mask,
                jnp.einsum(
                    "caju,iau->ajci", query_groups, key_segment, preferred_element_type=jnp.float32
                )
                * scale,
                NEG,
            )
            new_peak = jnp.maximum(peak, jnp.max(scores, axis=-1))
            weights = jnp.exp(scores - new_peak[..., None])
            factor = jnp.exp(peak - new_peak)
            total = total * factor + jnp.sum(weights, axis=-1)
            accum = accum * factor[..., None] + jnp.einsum(
                "xebw,wxy->xeby",
                weights.astype(jnp.bfloat16),
                v_piece,
                preferred_element_type=jnp.float32,
            )
            return (new_peak, total, accum)

        return lax.cond(needed, compute, lambda state: state, carry)

    init = (
        jnp.full((kv_local, repeat, tok_rows), NEG, jnp.float32),
        jnp.zeros((kv_local, repeat, tok_rows), jnp.float32),
        jnp.zeros((kv_local, repeat, tok_rows, head_dim), jnp.float32),
    )
    levels = (lax.axis_size("seq") // 2).bit_length() - 1
    window_k, window_v = (k_own, v_own)
    for level in range(levels):
        far_k, far_v = passed_along((window_k, window_v), "seq", 2**level)
        window_k = jnp.concatenate([far_k, window_k], axis=0)
        window_v = jnp.concatenate([far_v, window_v], axis=0)
    reach = 2**levels
    edge_k, edge_v = passed_along((k_own, v_own), "seq", reach)
    window_k = jnp.concatenate([edge_k, window_k], axis=0)
    window_v = jnp.concatenate([edge_v, window_v], axis=0)
    count = reach + 1
    base = anchor - reach * tok_rows

    def visit(step, state):
        piece_k = lax.dynamic_slice_in_dim(window_k, step * tok_rows, tok_rows, 0)
        piece_v = lax.dynamic_slice_in_dim(window_v, step * tok_rows, tok_rows, 0)
        return attend(state, (piece_k, piece_v), base + step * tok_rows)

    peak, total, accum = lax.fori_loop(0, count, visit, init)
    teacher = accum / total[..., None]
    k_grouped = k_own.reshape(tok_rows, kv_local, head_dim)
    value_groups = v_own.reshape(tok_rows, kv_local, head_dim)
    query_feature_map = feature_map(
        jnp.einsum(
            "tgrd,grdf->tgrf",
            query_groups,
            fq_weight.reshape(kv_local, repeat, head_dim, -1),
            preferred_element_type=jnp.float32,
        )
    )
    key_feature_map = feature_map(
        jnp.einsum(
            "tgd,grdf->tgrf",
            k_grouped,
            fk_weight.reshape(kv_local, repeat, head_dim, -1),
            preferred_element_type=jnp.float32,
        )
    )
    local_mask = (q_doc[:, None] == q_doc[None, :]) & (q_pos[None, :] <= q_pos[:, None])
    score_matrix = jnp.where(
        local_mask,
        jnp.einsum(
            "dbpj,zbpj->bpdz",
            query_feature_map,
            key_feature_map,
            preferred_element_type=jnp.float32,
        ),
        0.0,
    )
    numer = jnp.einsum(
        "xebw,wxy->xeby",
        score_matrix,
        value_groups.astype(jnp.float32),
        precision=lax.Precision.HIGHEST,
    )
    denom = jnp.sum(score_matrix, axis=-1)
    last_mask = (q_doc == q_doc[-1]).astype(jnp.bfloat16)
    phi_last = key_feature_map * last_mask[:, None, None, None]
    state = jnp.einsum("sgrf,sgd->grfd", phi_last, value_groups, preferred_element_type=jnp.float32)
    norm_state = jnp.sum(phi_last.astype(jnp.float32), axis=0)
    inside = jnp.sum(((starts >= anchor) & (starts < anchor + tok_rows)).astype(jnp.int32))
    keep = (inside == 0).astype(jnp.float32)
    identity = (jnp.ones((), jnp.float32), jnp.zeros_like(state), jnp.zeros_like(norm_state))
    running_prefix = entering((keep, state, norm_state), "seq", chain, identity)
    prev_doc = doc_index(jnp.reshape(anchor - 1, (1,)), starts)[0]
    carried = (q_doc == prev_doc).astype(jnp.float32)
    widened_feature_map = query_feature_map.astype(jnp.float32)
    numer = numer + carried[None, None, :, None] * jnp.einsum(
        "tgrf,grfd->grtd", widened_feature_map, running_prefix[1], precision=lax.Precision.HIGHEST
    )
    denom = denom + carried[None, None, :] * jnp.einsum(
        "skqa,kqa->kqs", widened_feature_map, running_prefix[2], precision=lax.Precision.HIGHEST
    )
    student = numer / denom[..., None]
    difference = teacher - student
    residual = jnp.transpose(difference, (2, 0, 1, 3)).reshape(tok_rows, heads * head_dim)
    local_loss = jnp.sum(jnp.mean(difference * difference, axis=-1), axis=(0, 1))
    token_loss = lax.psum(local_loss, "head")
    return (residual, token_loss)


def solution(mesh):
    in_specs = (
        P("seq", "head"),
        P("seq", None),
        P("seq", None),
        P(),
        P("head", None, None),
        P("head", None, None),
    )
    out_specs = (P("seq", "head"), P("seq"))
    return jax.shard_map(body, mesh=mesh, in_specs=in_specs, out_specs=out_specs, check_vma=False)
```

profile of v0, /device:TPU:7, one launch (start us, length us, event | category | flops | bytes accessed | tf_op | source)
XLA Modules:
  0.0 126.6 jit_solution(8340992441453852093)
XLA Ops:
  8.3 1.3 %copy.73 = bf16[2,8,128,128]{2,3,1,0:T(8,128)(2,1)S(1)} copy(bf16[2,8,128,128]{3,2,1,0:T(8,128)(2,1)} %bitcast.109) | data formatting | bytes 1048576 | tf_op jit(solution)/shard_map/reshape | solution.py:154
  17.2 1.5 %convolution_convert_fusion = bf16[2,8,256,128]{3,2,1,0:T(8,128)(2,1)} fusion(bf16[128,2,128,1]{0,2,3,1:T(8,128)(2,1)S(1)} %bitcast.106, bf16[128]{0:T(256)(128)(2,1)S(1)} %get-tuple-element.768, bf16[128,2,8,128]{0,3,2,1:T(8,128)(2,1)S(1)} %get-tuple-element.781, bf16[128,2,8,128]{0,3,2,1:T(8,128)(2,1)S(1)} %get-tuple-element.782), kind=kOutput, calls=%fused_computation.29 | convolution fusion | flops 137887744 | bytes 2162944 | tf_op jit(solution)/shard_map/sgrf,sgd->grfd/dot_general | solution.py:178
  26.6 1.5 %fusion.40 = (f32[2,8,128]{2,1,0:T(8,128)S(1)}, f32[2,8,128,128]{2,3,1,0:T(8,128)}) fusion(bf16[128,2,8,128]{0,3,2,1:T(8,128)(2,1)S(1)} %copy-done.6, bf16[128,2,8,128]{0,3,2,1:T(8,128)(2,1)S(1)} %copy-done.9, bf16[128,2,8,128]{0,3,2,1:T(8,128)(2,1)S(1)} %get-tuple-element.783, bf16[128,2,8,128]{0,3,2,1:T(8,128)(2,1)S(1)} %get-tuple-element.784, ...), kind=kOutput, calls=%fused_computation.87 | convolution fusion | flops 138934272 | bytes 3170304 | tf_op jit(solution)/shard_map/dbpj,zbpj->bpdz/dot_general | solution.py:161
  32.0 18.9 %all-reduce = bf16[8]{0:T(256)(128)(2,1)} all-reduce(bf16[8]{0:T(256)(128)(2,1)S(1)} %dynamic-update-slice), channel_id=1, replica_groups=mesh['seq'=8,'head'=4] {'seq'}, use_global_device_ids=true, to_apply=%add | all-reduce | flops 8 | bytes 32
  52.4 13.7 %all-gather.1 = bf16[16,8,256]{2,1,0:T(8,128)(2,1)S(1)} all-gather(bf16[2,8,256]{2,1,0:T(8,128)(2,1)S(1)} %multiply_reduce_fusion.1), channel_id=3, replica_groups=mesh['seq'=8,'head'=4] {'seq'}, dimensions={0}, use_global_device_ids=true | all-gather | bytes 73728 | tf_op jit(solution)/shard_map/all_gather | solution.py:22
  67.2 10.7 %while.37 = (s32[]{:T(128)}, f32[2,8,128]{2,1,0:T(8,128)S(1)}, f32[2,8,128]{2,1,0:T(8,128)S(1)}, f32[2,8,128,128]{3,2,1,0:T(8,128)S(1)}, s32[]{:T(128)}, /*index...) while((s32[]{:T(128)}, f32[2,8,128]{2,1,0:T(8,128)S(1)}, ...), condition=%wide.region_9.10_spmd.clone, body=%wide.region_3.9_spmd.clone.sunk | while | flops 136651776 | bytes 6331085 | solution.py:138
  67.8 1.5 %conditional.3 = ((f32[2,8,128]{2,1,0:T(8,128)S(1)}, f32[2,8,128]{2,1,0:T(8,128)S(1)}, f32[2,8,128,128]{3,2,1,0:T(8,128)S(1)})) conditional(s32[]{:T(128)} %convert_element_type.115, (f32[2,8,128]{2,1,0:T(8,128)S(1)}, f32[2,8,128]{2,1,0:T(8,128)S(1)}, f32[2,8,128,128]{3,2,1,0:T(8,128)S(1)}) %tuple.116, (s32[128]{0:T(128)S(1)}, s32[12]{0:T(128)S(1)}, ...), branch_computations={%region_4.4_spmd, %region_5.8_spmd} | conditional | flops 136651776 | bytes 6330242 | solution.py:113
  69.9 1.5 %conditional.3 = ((f32[2,8,128]{2,1,0:T(8,128)S(1)}, f32[2,8,128]{2,1,0:T(8,128)S(1)}, f32[2,8,128,128]{3,2,1,0:T(8,128)S(1)})) conditional(s32[]{:T(128)} %convert_element_type.115, (f32[2,8,128]{2,1,0:T(8,128)S(1)}, f32[2,8,128]{2,1,0:T(8,128)S(1)}, f32[2,8,128,128]{3,2,1,0:T(8,128)S(1)}) %tuple.116, (s32[128]{0:T(128)S(1)}, s32[12]{0:T(128)S(1)}, ...), branch_computations={%region_4.4_spmd, %region_5.8_spmd} | conditional | flops 136651776 | bytes 6330242 | solution.py:113
  72.1 1.5 %conditional.3 = ((f32[2,8,128]{2,1,0:T(8,128)S(1)}, f32[2,8,128]{2,1,0:T(8,128)S(1)}, f32[2,8,128,128]{3,2,1,0:T(8,128)S(1)})) conditional(s32[]{:T(128)} %convert_element_type.115, (f32[2,8,128]{2,1,0:T(8,128)S(1)}, f32[2,8,128]{2,1,0:T(8,128)S(1)}, f32[2,8,128,128]{3,2,1,0:T(8,128)S(1)}) %tuple.116, (s32[128]{0:T(128)S(1)}, s32[12]{0:T(128)S(1)}, ...), branch_computations={%region_4.4_spmd, %region_5.8_spmd} | conditional | flops 136651776 | bytes 6330242 | solution.py:113
  74.2 1.5 %conditional.3 = ((f32[2,8,128]{2,1,0:T(8,128)S(1)}, f32[2,8,128]{2,1,0:T(8,128)S(1)}, f32[2,8,128,128]{3,2,1,0:T(8,128)S(1)})) conditional(s32[]{:T(128)} %convert_element_type.115, (f32[2,8,128]{2,1,0:T(8,128)S(1)}, f32[2,8,128]{2,1,0:T(8,128)S(1)}, f32[2,8,128,128]{3,2,1,0:T(8,128)S(1)}) %tuple.116, (s32[128]{0:T(128)S(1)}, s32[12]{0:T(128)S(1)}, ...), branch_computations={%region_4.4_spmd, %region_5.8_spmd} | conditional | flops 136651776 | bytes 6330242 | solution.py:113
  76.3 1.5 %conditional.3 = ((f32[2,8,128]{2,1,0:T(8,128)S(1)}, f32[2,8,128]{2,1,0:T(8,128)S(1)}, f32[2,8,128,128]{3,2,1,0:T(8,128)S(1)})) conditional(s32[]{:T(128)} %convert_element_type.115, (f32[2,8,128]{2,1,0:T(8,128)S(1)}, f32[2,8,128]{2,1,0:T(8,128)S(1)}, f32[2,8,128,128]{3,2,1,0:T(8,128)S(1)}) %tuple.116, (s32[128]{0:T(128)S(1)}, s32[12]{0:T(128)S(1)}, ...), branch_computations={%region_4.4_spmd, %region_5.8_spmd} | conditional | flops 136651776 | bytes 6330242 | solution.py:113
  77.9 1.3 %copy.69 = f32[2,8,128,128]{2,3,1,0:T(8,128)} copy(f32[2,8,128,128]{3,2,1,0:T(8,128)S(1)} %get-tuple-element.616) | data formatting | bytes 2097152 | tf_op jit(solution)/shard_map/while | solution.py:138
  80.1 23.6 %while.36 = (s32[]{:T(128)}, f32[2,8,256,128]{3,2,1,0:T(8,128)S(1)}, f32[2,8,256]{2,1,0:T(8,128)S(1)}, s32[]{:T(128)}, bf16[8,2,8,256,128]{4,3,2,1,0:T(8,128)(2,...) while((s32[]{:T(128)}, ...), condition=%wide.region_22.23_spmd, body=%wide.region_21.22_spmd.sunk | while | flops 1585158 | bytes 5284005 | solution.py:38
  81.4 2.1 %convert_add_fusion.4 = f32[2,8,256,128]{3,2,1,0:T(8,128)S(1)} fusion(f32[2,8,256,128]{3,2,1,0:T(8,128)S(1)} %get-tuple-element.931, f32[]{:T(128)S(6)} %convert.49, bf16[8,2,8,256,128]{4,3,2,1,0:T(8,128)(2,1)} %get-tuple-element.944, s32[]{:T(128)S(6)} %select_n.55), kind=kLoop, calls=%fused_computation.19.clone.1 | loop fusion | flops 1572864 | bytes 5242888 | tf_op jit(solution)/shard_map/while/body/add | solution.py:54
  84.7 2.1 %convert_add_fusion.4 = f32[2,8,256,128]{3,2,1,0:T(8,128)S(1)} fusion(f32[2,8,256,128]{3,2,1,0:T(8,128)S(1)} %get-tuple-element.931, f32[]{:T(128)S(6)} %convert.49, bf16[8,2,8,256,128]{4,3,2,1,0:T(8,128)(2,1)} %get-tuple-element.944, s32[]{:T(128)S(6)} %select_n.55), kind=kLoop, calls=%fused_computation.19.clone.1 | loop fusion | flops 1572864 | bytes 5242888 | tf_op jit(solution)/shard_map/while/body/add | solution.py:54
  88.1 2.1 %convert_add_fusion.4 = f32[2,8,256,128]{3,2,1,0:T(8,128)S(1)} fusion(f32[2,8,256,128]{3,2,1,0:T(8,128)S(1)} %get-tuple-element.931, f32[]{:T(128)S(6)} %convert.49, bf16[8,2,8,256,128]{4,3,2,1,0:T(8,128)(2,1)} %get-tuple-element.944, s32[]{:T(128)S(6)} %select_n.55), kind=kLoop, calls=%fused_computation.19.clone.1 | loop fusion | flops 1572864 | bytes 5242888 | tf_op jit(solution)/shard_map/while/body/add | solution.py:54
  91.5 2.1 %convert_add_fusion.4 = f32[2,8,256,128]{3,2,1,0:T(8,128)S(1)} fusion(f32[2,8,256,128]{3,2,1,0:T(8,128)S(1)} %get-tuple-element.931, f32[]{:T(128)S(6)} %convert.49, bf16[8,2,8,256,128]{4,3,2,1,0:T(8,128)(2,1)} %get-tuple-element.944, s32[]{:T(128)S(6)} %select_n.55), kind=kLoop, calls=%fused_computation.19.clone.1 | loop fusion | flops 1572864 | bytes 5242888 | tf_op jit(solution)/shard_map/while/body/add | solution.py:54
  94.9 2.1 %convert_add_fusion.4 = f32[2,8,256,128]{3,2,1,0:T(8,128)S(1)} fusion(f32[2,8,256,128]{3,2,1,0:T(8,128)S(1)} %get-tuple-element.931, f32[]{:T(128)S(6)} %convert.49, bf16[8,2,8,256,128]{4,3,2,1,0:T(8,128)(2,1)} %get-tuple-element.944, s32[]{:T(128)S(6)} %select_n.55), kind=kLoop, calls=%fused_computation.19.clone.1 | loop fusion | flops 1572864 | bytes 5242888 | tf_op jit(solution)/shard_map/while/body/add | solution.py:54
  98.2 2.1 %convert_add_fusion.4 = f32[2,8,256,128]{3,2,1,0:T(8,128)S(1)} fusion(f32[2,8,256,128]{3,2,1,0:T(8,128)S(1)} %get-tuple-element.931, f32[]{:T(128)S(6)} %convert.49, bf16[8,2,8,256,128]{4,3,2,1,0:T(8,128)(2,1)} %get-tuple-element.944, s32[]{:T(128)S(6)} %select_n.55), kind=kLoop, calls=%fused_computation.19.clone.1 | loop fusion | flops 1572864 | bytes 5242888 | tf_op jit(solution)/shard_map/while/body/add | solution.py:54
  101.6 2.1 %convert_add_fusion.4 = f32[2,8,256,128]{3,2,1,0:T(8,128)S(1)} fusion(f32[2,8,256,128]{3,2,1,0:T(8,128)S(1)} %get-tuple-element.931, f32[]{:T(128)S(6)} %convert.49, bf16[8,2,8,256,128]{4,3,2,1,0:T(8,128)(2,1)} %get-tuple-element.944, s32[]{:T(128)S(6)} %select_n.55), kind=kLoop, calls=%fused_computation.19.clone.1 | loop fusion | flops 1572864 | bytes 5242888 | tf_op jit(solution)/shard_map/while/body/add | solution.py:54
  103.8 1.6 %fusion.26 = f32[2,8,1,128]{3,2,1,0:T(1,128)S(1)} fusion(bf16[128,2,8,128]{0,3,2,1:T(8,128)(2,1)S(1)} %copy-done.2, bf16[128,2,8,128]{0,3,2,1:T(8,128)(2,1)} %copy-done.3, f32[2,8,256,1]{2,1,0,3:T(8,128)S(1)} %bitcast.108), kind=kOutput, calls=%fused_computation.57 | convolution fusion | flops 8388608 | bytes 1073152 | tf_op jit(solution)/shard_map/skqa,kqa->kqs/dot_general | solution.py:190
  105.4 1.9 %convolution_multiply_fusion.1 = f32[2,8,128,128]{2,3,1,0:T(8,128)S(1)} fusion(f32[2,8,256,128]{3,2,1,0:T(8,128)S(1)} %get-tuple-element.618, f32[128]{0:T(128)S(1)} %get-tuple-element.767, bf16[128,2,8,128]{0,3,2,1:T(8,128)(2,1)S(1)} %copy-done.2, bf16[128,2,8,128]{0,3,2,1:T(8,128)(2,1)S(1)} %copy-done.4), kind=kOutput, calls=%fused_computation.34 | convolution fusion | flops 807665664 | bytes 4194816 | tf_op jit(solution)/shard_map/tgrf,grfd->grtd/dot_general | solution.py:187
  108.3 1.3 %copy.80 = f32[128,2048]{1,0:T(8,128)} copy(f32[128,2048]{0,1:T(8,128)S(1)} %bitcast.105) | data formatting | bytes 2097152
  109.6 10.2 %psum.7 = f32[128]{0:T(128)} all-reduce(f32[128]{0:T(128)S(1)} %multiply_reduce_fusion.2), channel_id=1, replica_groups=mesh['seq'=8,'head'=4] {'head'}, use_global_device_ids=true, to_apply=%region_26.27 | all-reduce | flops 128 | bytes 1024 | tf_op jit(solution)/shard_map/psum | solution.py:197
  (169 shorter events, 35.1 us)
Async XLA Ops:
  7.2 17.2 %copy-start = (bf16[16,128,128]{2,1,0:T(8,128)(2,1)S(1)}, bf16[16,128,128]{2,1,0:T(8,128)(2,1)}, u32[]{:S(2)}) copy-start(bf16[16,128,128]{2,1,0:T(8,128)(2,1)} %param.16) | copy-start | bytes 1572868
  7.2 72.7 %all-gather.4.cloned.1.call-start = ((), (), s32[]{:S(2)}) async-start(), calls=%async_computation | async-start | bytes 9437184 | tf_op jit(solution)/shard_map/all_gather | solution.py:22
  9.9 3.2 %copy-start.13 = (s32[12]{0:T(128)S(1)}, s32[12]{0:T(128)}, u32[]{:S(2)}) copy-start(s32[12]{0:T(128)} %param.15) | copy-start | bytes 148
  13.9 4.8 %copy-start.14 = (s32[12]{0:T(128)}, s32[12]{0:T(128)S(1)}, u32[]{:S(2)}) copy-start(s32[12]{0:T(128)S(1)} %get-tuple-element.958) | copy-start | bytes 148
  16.2 7.7 %copy-start.12 = (bf16[128,2048]{1,0:T(8,128)(2,1)S(1)}, bf16[128,2048]{1,0:T(8,128)(2,1)}, u32[]{:S(2)}) copy-start(bf16[128,2048]{1,0:T(8,128)(2,1)} %param.12) | copy-start | bytes 1572868
  18.7 11.3 %collective-permute-start.1 = (bf16[128,256]{0,1:T(8,128)(2,1)S(1)}, bf16[128,256]{0,1:T(8,128)(2,1)S(1)}, u32[]{:S(2)}, u32[]{:S(2)}) collective-permute-start(bf16[128,256]{0,1:T(8,128)(2,1)S(1)} %copy.102), channel_id=1, source_target_pairs={{0,4},{4,8},{8,12},{12,16},{16,20},{20,24},{24,28},{1,5},{5,9},{9,... | collective-permute-start | bytes 196616 | tf_op jit(solution)/shard_map/ppermute | solution.py:16
  20.0 46.1 %collective-permute-start = (bf16[128,256]{0,1:T(8,128)(2,1)S(1)}, bf16[128,256]{0,1:T(8,128)(2,1)}, u32[]{:S(2)}, u32[]{:S(2)}) collective-permute-start(bf16[128,256]{0,1:T(8,128)(2,1)S(1)} %copy.102), channel_id=1, source_target_pairs={{0,16},{4,20},{8,24},{12,28},{1,17},{5,21},{9,25},{13,29},{2,18},{... | collective-permute-start | bytes 196616 | tf_op jit(solution)/shard_map/ppermute | solution.py:16
  21.3 29.8 %collective-permute-start.4 = (bf16[128,256]{0,1:T(8,128)(2,1)S(1)}, bf16[128,256]{0,1:T(8,128)(2,1)S(1)}, u32[]{:S(2)}, u32[]{:S(2)}) collective-permute-start(bf16[128,256]{0,1:T(8,128)(2,1)S(1)} %copy.103), channel_id=1, source_target_pairs={{0,4},{4,8},{8,12},{12,16},{16,20},{20,24},{24,28},{1,5},{5,9},{9,... | collective-permute-start | bytes 196616 | tf_op jit(solution)/shard_map/ppermute | solution.py:16
  22.6 44.4 %collective-permute-start.3 = (bf16[128,256]{0,1:T(8,128)(2,1)S(1)}, bf16[128,256]{0,1:T(8,128)(2,1)S(1)}, u32[]{:S(2)}, u32[]{:S(2)}) collective-permute-start(bf16[128,256]{0,1:T(8,128)(2,1)S(1)} %copy.103), channel_id=1, source_target_pairs={{0,16},{4,20},{8,24},{12,28},{1,17},{5,21},{9,25},{13,29},{2,18},{... | collective-permute-start | bytes 196616 | tf_op jit(solution)/shard_map/ppermute | solution.py:16
  25.3 1.0 copy-start.6
  25.3 1.2 copy-start.9
  25.6 2.4 %copy-start.1 = (bf16[128,2,8,128]{0,3,2,1:T(8,128)(2,1)}, bf16[128,2,8,128]{0,3,2,1:T(8,128)(2,1)S(1)}, u32[]{:S(2)}) copy-start(bf16[128,2,8,128]{0,3,2,1:T(8,128)(2,1)S(1)} %get-tuple-element.783) | copy-start | bytes 1572868
  25.6 2.4 %copy-start.3 = (bf16[128,2,8,128]{0,3,2,1:T(8,128)(2,1)}, bf16[128,2,8,128]{0,3,2,1:T(8,128)(2,1)S(1)}, u32[]{:S(2)}) copy-start(bf16[128,2,8,128]{0,3,2,1:T(8,128)(2,1)S(1)} %get-tuple-element.784) | copy-start | bytes 1572868
  26.6 2.1 %copy-start.17 = (u32[32]{0:T(128)S(1)}, u32[32]{0:T(128)}, u32[]{:S(2)}) copy-start(u32[32]{0:T(128)} %constant.182) | copy-start | bytes 388
  26.6 4.7 %copy-start.7 = (bf16[128,2,8,128]{0,3,2,1:T(8,128)(2,1)S(1)}, bf16[128,2,8,128]{0,3,2,1:T(8,128)(2,1)}, u32[]{:S(2)}) copy-start(bf16[128,2,8,128]{0,3,2,1:T(8,128)(2,1)} %copy-done.5) | copy-start | bytes 1572868
  26.6 4.8 %copy-start.10 = (bf16[128,2,8,128]{0,3,2,1:T(8,128)(2,1)S(1)}, bf16[128,2,8,128]{0,3,2,1:T(8,128)(2,1)}, u32[]{:S(2)}) copy-start(bf16[128,2,8,128]{0,3,2,1:T(8,128)(2,1)} %copy-done.8) | copy-start | bytes 1572868
  30.0 36.1 %collective-permute-start.2 = (bf16[256,256]{0,1:T(8,128)(2,1)S(1)}, bf16[256,256]{0,1:T(8,128)(2,1)S(1)}, u32[]{:S(2)}, u32[]{:S(2)}) collective-permute-start(bf16[256,256]{0,1:T(8,128)(2,1)S(1)} %pad_maximum_fusion.9), channel_id=1, source_target_pairs={{0,8},{4,12},{8,16},{12,20},{16,24},{20,28},{1,9},{5,13},{9,17},{1... | collective-permute-start | bytes 393224 | tf_op jit(solution)/shard_map/ppermute | solution.py:16
  31.9 35.2 %copy-start.15 = (s32[12]{0:T(128)S(1)}, s32[12]{0:T(128)}, u32[]{:S(2)}) copy-start(s32[12]{0:T(128)} %copy-done.14) | copy-start | bytes 148
  51.1 15.9 %collective-permute-start.5 = (bf16[256,256]{0,1:T(8,128)(2,1)S(1)}, bf16[256,256]{0,1:T(8,128)(2,1)S(1)}, u32[]{:S(2)}, u32[]{:S(2)}) collective-permute-start(bf16[256,256]{0,1:T(8,128)(2,1)S(1)} %pad_maximum_fusion.10), channel_id=1, source_target_pairs={{0,8},{4,12},{8,16},{12,20},{16,24},{20,28},{1,9},{5,13},{9,17},{1... | collective-permute-start | bytes 393224 | tf_op jit(solution)/shard_map/ppermute | solution.py:16
  77.9 2.2 %copy-start.16 = (bf16[8]{0:T(256)(128)(2,1)S(1)}, bf16[8]{0:T(256)(128)(2,1)}, u32[]{:S(2)}) copy-start(bf16[8]{0:T(256)(128)(2,1)} %all-reduce) | copy-start | bytes 52
  80.1 23.7 %copy-start.2 = (bf16[128,2,8,128]{0,3,2,1:T(8,128)(2,1)S(1)}, bf16[128,2,8,128]{0,3,2,1:T(8,128)(2,1)}, u32[]{:S(2)}) copy-start(bf16[128,2,8,128]{0,3,2,1:T(8,128)(2,1)} %copy-done.1) | copy-start | bytes 1572868
  103.7 1.6 %copy-start.4 = (bf16[128,2,8,128]{0,3,2,1:T(8,128)(2,1)S(1)}, bf16[128,2,8,128]{0,3,2,1:T(8,128)(2,1)}, u32[]{:S(2)}) copy-start(bf16[128,2,8,128]{0,3,2,1:T(8,128)(2,1)} %copy-done.3) | copy-start | bytes 1572868
  105.4 2.0 %copy-start.11 = (f32[2,8,128,128]{2,3,1,0:T(8,128)S(1)}, f32[2,8,128,128]{2,3,1,0:T(8,128)}, u32[]{:S(2)}) copy-start(f32[2,8,128,128]{2,3,1,0:T(8,128)} %copy.69) | copy-start | bytes 3145732
  105.4 2.0 %copy-start.18 = (f32[2,8,128,128]{2,3,1,0:T(8,128)S(1)}, f32[2,8,128,128]{2,3,1,0:T(8,128)}, u32[]{:S(2)}) copy-start(f32[2,8,128,128]{2,3,1,0:T(8,128)} %get-tuple-element.778) | copy-start | bytes 3145732
  (2 other events, 1.8 us)
Sparse Core Ops, SparseCore 0:
  18.8 60.9 all-gather.3
where the time goes:
time: 127 us
  blocking collectives  42.7 us (34%)
  other arithmetic  22.8 us (18%)
  between operations  15.8 us (12%)
  local copies, waits for them, and re-layouts  15.1 us (12%)
  matrix products  13.8 us (11%)
  loops' own time  7.96 us (6%)
  starting transfers between devices  7.79 us (6%)
    unnamed x1, blocking collectives  18.9 us
    add x7, other arithmetic, chain(): later[1] + later[0] * earlier[1]  14.7 us
    all_gather x1, blocking collectives, entering(): lax.all_gather(a.astype(kind), axis)  13.7 us
    psum x1, blocking collectives, body(): token_loss = lax.psum(local_loss, 'head')  10.2 us
    ppermute x6, starting transfers between devices, passed_along(): return lax.ppermute(block, axis, route)  7.75 us
    unnamed x46, local copies, waits for them, and re-layouts  5.41 us
    another operation x1, loops' own time, entering(): return lax.fori_loop(0, place, one, state)  4.55 us
    dynamic_slice x7, local copies, waits for them, and re-layouts, one(): lax.dynamic_index_in_dim(a, turn, 0, False).astype(own.dtype)  4.33 us
  transfers between devices with their start and end apart: 7, of which 1 were waited for; matrix products, arithmetic and copies ran while one was open for 12% of the time, Pallas kernels for 0%

commit v1 on v0

v1 whole, which is shorter than its diff:
```python
import functools

import jax
import jax.numpy as jnp
from jax import lax
from jax.experimental import pallas as pl
from jax.experimental.pallas import tpu as pltpu
from jax.sharding import PartitionSpec as P

QH = 64
KVH = 8
NEG = -1e30
MESH = pl.DeviceIdType.MESH
UNROLL = 2


def kernel(
    n, nh, dl, q_hbm, k_hbm, v_hbm, fq_hbm, fk_hbm, res, loss,
    q, fq, fk, fkt, kv, kt, vx, phiq, acc, peak, qstart, sq, lbuf, lrecv,
    lsem, osem, ssem, rsem, lssem, lrsem,
):
    T = q_hbm.shape[0]
    H, D, F = fq_hbm.shape
    KV = kv.shape[1]
    G = H // KV
    group = QH // KVH
    reach = n // 2
    E = reach // 2
    s = lax.axis_index("seq")
    z = lax.axis_index("head")
    core = lax.rem(s, 2)
    partner = s + 1 - 2 * core
    kv_first = z * H // group
    src = (k_hbm, v_hbm)

    def own(i, g):
        col = pl.multiple_of((kv_first + g) * D, D)
        return src[i].at[:, pl.ds(col, D)]

    load_q = pltpu.make_async_copy(q_hbm, q, lsem.at[0])
    load_fq = pltpu.make_async_copy(fq_hbm, fq, lsem.at[1])
    load_fk = pltpu.make_async_copy(fk_hbm, fk, lsem.at[2])
    own_loads = [
        [pltpu.make_async_copy(own(i, g), kv.at[i, g, 0], osem.at[i, g]) for g in range(KV)]
        for i in range(2)
    ]

    barrier = pltpu.get_barrier_semaphore()
    pl.semaphore_signal(barrier, inc=1, device_id=(partner, z), device_id_type=MESH)
    for e in range(1, E + 1):
        @pl.when(s + 2 * e < n)
        def _():
            pl.semaphore_signal(barrier, inc=1, device_id=(s + 2 * e, z), device_id_type=MESH)

        @pl.when(s - 2 * e >= 0)
        def _():
            pl.semaphore_signal(barrier, inc=1, device_id=(s - 2 * e, z), device_id_type=MESH)
    for e in range(1, nh):
        pl.semaphore_signal(barrier, inc=1, device_id=(s, lax.rem(z + e, nh)), device_id_type=MESH)

    load_q.start()
    load_fq.start()
    load_fk.start()
    for g in range(KV):
        for i in range(2):
            own_loads[i][g].start()

    def direct(i, g, e):
        return pltpu.make_async_remote_copy(
            src_ref=own(i, g), dst_ref=kv.at[i, g, 2 * e],
            send_sem=ssem.at[i, g, 2 * e], recv_sem=rsem.at[i, g, 2 * e],
            device_id=(s + 2 * e, z), device_id_type=MESH)

    def to_partner(i, g):
        return pltpu.make_async_remote_copy(
            src_ref=own(i, g), dst_ref=kv.at[i, g, 1],
            send_sem=ssem.at[i, g, 1], recv_sem=rsem.at[i, g, 1],
            device_id=(partner, z), device_id_type=MESH)

    def relay(i, g, e, k):
        d = 2 * e + 1 - 2 * k
        return pltpu.make_async_remote_copy(
            src_ref=kv.at[i, g, 2 * e], dst_ref=kv.at[i, g, d],
            send_sem=ssem.at[i, g, d], recv_sem=rsem.at[i, g, d],
            device_id=(partner, z), device_id_type=MESH)

    def arrived(i, g, d):
        return pltpu.make_async_remote_copy(
            src_ref=kv.at[i, g, d], dst_ref=kv.at[i, g, d],
            send_sem=ssem.at[i, g, d], recv_sem=rsem.at[i, g, d],
            device_id=(partner, z), device_id_type=MESH)

    anchor = s * T
    qpos = anchor + lax.broadcasted_iota(jnp.int32, (T, 2 * T), 0)
    first = jnp.zeros((T, 2 * T), jnp.int32)
    run = jnp.int32(0)
    for i in range(dl.shape[0]):
        first = jnp.where(qpos >= run, run, first)
        run = run + dl[i]
    qstart[...] = first

    for d in range(1, reach + 1):
        @pl.when(s < d)
        def _():
            kv[:, :, d] = jnp.zeros((2, KV, T, D), kv.dtype)

    pl.semaphore_wait(barrier, 1 + (nh - 1) + jnp.minimum(E, (n - 1 - s) // 2) + jnp.minimum(E, s // 2))

    @pl.when(core == 0)
    def _():
        for g in range(KV):
            for i in range(2):
                to_partner(i, g).start()
    for e in range(1, E + 1):
        @pl.when(s + 2 * e < n)
        def _():
            for g in range(KV):
                for i in range(2):
                    direct(i, g, e).start()

    def qh(h):
        return q[:, pl.ds(pl.multiple_of(h * D, D), D)]

    load_q.wait()
    load_fq.wait()
    load_fk.wait()

    def prepare(h):
        p = jnp.dot(qh(h), fq[h], preferred_element_type=jnp.float32)
        e1 = jnp.exp(p - jnp.max(p, axis=1, keepdims=True))
        e2 = jnp.exp(jnp.min(p, axis=1, keepdims=True) - p)
        e1 = e1 / jnp.sum(e1, axis=1, keepdims=True)
        e2 = e2 / jnp.sum(e2, axis=1, keepdims=True)
        phiq[h] = jnp.concatenate([e1, e2], axis=1).astype(jnp.bfloat16)
        fkt[h] = fk[h].T

    def heads_loop(lo, hi, fn):
        def step(t, c):
            for u in range(UNROLL):
                fn(lo + t * UNROLL + u)
            return c

        lax.fori_loop(0, (hi - lo) // UNROLL, step, 0)

    heads_loop(0, H, prepare)
    sq[...] = jnp.zeros_like(sq)
    c = (D ** -0.5) * 1.4426950408889634

    def chunk(g, ds, last):
        W = T * len(ds)
        initial = ds[0] == 0
        for j, d in enumerate(ds):
            kt[g, :, pl.ds(j * T, T)] = kv[0, g, d].T
            vx[g, pl.ds(j * T, T), pl.ds(0, D)] = kv[1, g, d]
        kpos = lax.broadcasted_iota(jnp.int32, (T, W), 1)
        if initial:
            kpos = kpos + anchor
        else:
            kpos = anchor - ds[0] * T + jnp.where(kpos >= T, kpos - 2 * T, kpos)

        def one(h):
            mask = kpos >= qstart[:, pl.ds(0, W)]
            if initial:
                row = anchor + lax.broadcasted_iota(jnp.int32, (T, W), 0)
                mask = mask & (kpos <= row)
            kth = kt[g, :, pl.ds(0, W)]
            sc = jnp.dot(qh(h), kth, preferred_element_type=jnp.float32)
            sc = jnp.where(mask, sc, NEG)
            top = jnp.max(sc, axis=1, keepdims=True)
            if not initial:
                old = peak[h]
                new = jnp.maximum(old, top)
                factor = jnp.exp2((old - new) * c)
                sub = jnp.concatenate([new, new], axis=1)
            else:
                new = jnp.broadcast_to(top, (T, D))
                sub = new
            w = jnp.exp2((sc - sub) * c).astype(jnp.bfloat16)
            p = jnp.dot(fkt[h], kth, preferred_element_type=jnp.float32)
            e1 = jnp.exp(p - jnp.max(p, axis=0, keepdims=True))
            e2 = jnp.exp(jnp.min(p, axis=0, keepdims=True) - p)
            e1 = e1 * (1.0 / jnp.sum(e1, axis=0, keepdims=True))
            e2 = e2 * (1.0 / jnp.sum(e2, axis=0, keepdims=True))
            phik = jnp.concatenate([e1, e2], axis=0).astype(jnp.bfloat16)
            aff = jnp.dot(phiq[h], phik, preferred_element_type=jnp.float32)
            aff = jnp.where(mask, aff, 0.0).astype(jnp.bfloat16)
            vxg = vx[g, pl.ds(0, W)]
            ot = jnp.dot(w, vxg, preferred_element_type=jnp.float32)
            os = jnp.dot(aff, vxg, preferred_element_type=jnp.float32)
            if not initial:
                ot = ot + acc[h, pl.ds(0, T)] * jnp.concatenate([factor, factor], axis=1)
                os = os + acc[h, pl.ds(T, T)]
            if last:
                r = ot[:, :D] / ot[:, D:] - os[:, :D] / os[:, D:]
                res[:, pl.ds(pl.multiple_of(h * D, D), D)] = r
                sq[...] += r * r
            else:
                peak[h] = new
                acc[h, pl.ds(0, T)] = ot
                acc[h, pl.ds(T, T)] = os

        heads_loop(g * G, (g + 1) * G, one)

    for g in range(KV):
        vx[g, :, pl.ds(D, D)] = jnp.ones((2 * T, D), vx.dtype)
    for g in range(KV):
        for i in range(2):
            own_loads[i][g].wait()
        chunk(g, (0,), False)

    def pass_on(g, e):
        @pl.when(s >= 2 * e)
        def _():
            for i in range(2):
                arrived(i, g, 2 * e).wait_recv()

        for k in range(2):
            if 2 * e + 1 - 2 * k <= reach:
                @pl.when((s >= 2 * e) & (core == k))
                def _():
                    for i in range(2):
                        relay(i, g, e, k).start()

    for e in range(1, E + 1):
        for g in range(KV):
            pass_on(g, e)
        for g in range(KV):
            @pl.when(s >= 2 * e - 1)
            def _():
                for i in range(2):
                    arrived(i, g, 2 * e - 1).wait_recv()
            chunk(g, (2 * e - 1, 2 * e), e == E)

    part = jnp.sum(sq[...].T, axis=0, keepdims=True) * (1.0 / D)
    lbuf[...] = jnp.broadcast_to(part, lbuf.shape)

    def send_loss(e):
        return pltpu.make_async_remote_copy(
            src_ref=lbuf, dst_ref=lrecv.at[e], send_sem=lssem.at[e], recv_sem=lrsem.at[e],
            device_id=(s, lax.rem(z + e, nh)), device_id_type=MESH)

    for e in range(1, nh):
        send_loss(e).start()

    @pl.when(core == 0)
    def _():
        for g in range(KV):
            for i in range(2):
                to_partner(i, g).wait_send()
    for e in range(1, E + 1):
        @pl.when(s + 2 * e < n)
        def _():
            for g in range(KV):
                for i in range(2):
                    direct(i, g, e).wait_send()
        for k in range(2):
            if 2 * e + 1 - 2 * k <= reach:
                @pl.when((s >= 2 * e) & (core == k))
                def _():
                    for g in range(KV):
                        for i in range(2):
                            relay(i, g, e, k).wait_send()
    total = lbuf[0:1]
    for e in range(1, nh):
        send_loss(e).wait_send()
        send_loss(e).wait_recv()
        total = total + lrecv[e, 0:1]
    loss[...] = total


def body(queries, keys, values, doc_lengths, fq_weight, fk_weight):
    n = lax.axis_size("seq")
    nh = lax.axis_size("head")
    T = queries.shape[0]
    H, D, F = fq_weight.shape
    KV = max(1, H // (QH // KVH))
    reach = n // 2
    bf, f32 = jnp.bfloat16, jnp.float32
    hbm = pl.BlockSpec(memory_space=pl.ANY)
    vm = pl.BlockSpec(memory_space=pltpu.VMEM)
    DMA = pltpu.SemaphoreType.DMA
    res, loss = pl.pallas_call(
        functools.partial(kernel, n, nh),
        out_shape=(
            jax.ShapeDtypeStruct((T, H * D), f32),
            jax.ShapeDtypeStruct((1, T), f32),
        ),
        in_specs=[pl.BlockSpec(memory_space=pltpu.SMEM)] + [hbm] * 5,
        out_specs=(vm, vm),
        scratch_shapes=[
            pltpu.VMEM((T, H * D), bf),
            pltpu.VMEM((H, D, F), bf),
            pltpu.VMEM((H, D, F), bf),
            pltpu.VMEM((H, F, D), bf),
            pltpu.VMEM((2, KV, reach + 1, T, D), bf),
            pltpu.VMEM((KV, D, 2 * T), bf),
            pltpu.VMEM((KV, 2 * T, 2 * D), bf),
            pltpu.VMEM((H, T, 2 * F), bf),
            pltpu.VMEM((H, 2 * T, 2 * D), f32),
            pltpu.VMEM((H, T, D), f32),
            pltpu.VMEM((T, 2 * T), jnp.int32),
            pltpu.VMEM((T, D), f32),
            pltpu.VMEM((8, T), f32),
            pltpu.VMEM((nh, 8, T), f32),
            DMA((3,)),
            DMA((2, KV)),
            DMA((2, KV, reach + 1)),
            DMA((2, KV, reach + 1)),
            DMA((nh,)),
            DMA((nh,)),
        ],
        compiler_params=pltpu.CompilerParams(
            collective_id=0, has_side_effects=True, vmem_limit_bytes=40 * 1024 * 1024
        ),
    )(doc_lengths, queries, keys, values, fq_weight, fk_weight)
    return res, loss.reshape(T)


def solution(mesh):
    in_specs = (
        P("seq", "head"),
        P("seq", None),
        P("seq", None),
        P(),
        P("head", None, None),
        P("head", None, None),
    )
    out_specs = (P("seq", "head"), P("seq"))
    return jax.shard_map(body, mesh=mesh, in_specs=in_specs, out_specs=out_specs, check_vma=False)
```

time: 127 us -> 42.6 us (0.34)
  the two profiles are of different devices: /device:TPU:7 before, /device:TPU:0 now
where the time goes in v1:
time: 42.6 us; the launch traced here: 42.3 us
  Pallas kernels  34.5 us (81%)
  local copies, waits for them, and re-layouts  7.15 us (17%)
  between operations  0.65 us (2%)
    pallas_call x1, Pallas kernels, body(): pl.pallas_call(functools.partial(kernel, n, nh), out_shape=(jax.ShapeDtyp...  34.5 us
    unnamed x14, local copies, waits for them, and re-layouts  7.15 us

profile of v1, /device:TPU:0, one launch (start us, length us, event | category | flops | bytes accessed | tf_op | source)
XLA Modules:
  0.0 42.3 jit_solution(2564249578453841610)
XLA Ops:
  0.6 0.0 copy-start
  0.6 1.0 %copy-done = bf16[128,2048]{1,0:T(8,128)(2,1)S(1)} copy-done((bf16[128,2048]{1,0:T(8,128)(2,1)S(1)}, bf16[128,2048]{1,0:T(8,128)(2,1)}, u32[]{:S(2)}) %copy-start) | copy-done | bytes 524312
  1.7 0.0 copy-start.1
  1.7 1.0 %copy-done.1 = bf16[16,128,128]{2,1,0:T(8,128)(2,1)S(1)} copy-done((bf16[16,128,128]{2,1,0:T(8,128)(2,1)S(1)}, bf16[16,128,128]{2,1,0:T(8,128)(2,1)}, u32[]{:S(2)}) %copy-start.1) | copy-done | bytes 524312
  2.7 0.0 copy-start.2
  2.7 1.0 %copy-done.2 = bf16[16,128,128]{2,1,0:T(8,128)(2,1)S(1)} copy-done((bf16[16,128,128]{2,1,0:T(8,128)(2,1)S(1)}, bf16[16,128,128]{2,1,0:T(8,128)(2,1)}, u32[]{:S(2)}) %copy-start.2) | copy-done | bytes 524312
  3.8 0.0 copy-start.3
  3.8 0.9 %copy-done.3 = bf16[128,1024]{1,0:T(8,128)(2,1)S(1)} copy-done((bf16[128,1024]{1,0:T(8,128)(2,1)S(1)}, bf16[128,1024]{1,0:T(8,128)(2,1)}, u32[]{:S(2)}) %copy-start.3) | copy-done | bytes 262168
  4.7 0.0 copy-start.4
  4.7 0.9 %copy-done.4 = bf16[128,1024]{1,0:T(8,128)(2,1)S(1)} copy-done((bf16[128,1024]{1,0:T(8,128)(2,1)S(1)}, bf16[128,1024]{1,0:T(8,128)(2,1)}, u32[]{:S(2)}) %copy-start.4) | copy-done | bytes 262168
  5.7 0.0 copy-start.5
  5.7 0.7 %copy-done.5 = s32[12]{0:T(128)S(1)} copy-done((s32[12]{0:T(128)S(1)}, s32[12]{0:T(128)}, u32[]{:S(2)}) %copy-start.5) | copy-done | bytes 72
  6.3 34.5 %shard_map.77 = (f32[128,2048]{1,0:T(8,128)S(1)}, f32[1,128]{1,0:T(1,128)S(1)}) custom-call(s32[12]{0:T(128)S(1)} %copy-done.5, bf16[128,2048]{1,0:T(8,128)(2,1)S(1)} %copy-done, bf16[128,1024]{1,0:T(8,128)(2,1)S(1)} %copy-done.3, bf16[128,1024]{1,0:T(8,128)(2,1)S(1)} %copy-done.4, bf16[16,128,128]{2,1,0:T(8,128)(2,1)S(1)} %copy-done.1, ...), custom_call_target="tpu_custom_call" | custom-call | tf_op jit(solution)/shard_map/pallas_call | solution.py:282
  40.8 1.0 %copy.10 = f32[128,2048]{1,0:T(8,128)} copy(f32[128,2048]{1,0:T(8,128)S(1)} %get-tuple-element.8) | data formatting | bytes 2097152
  41.8 0.5 %copy.11 = f32[128]{0:T(128)} copy(f32[128]{0:T(128)S(1)} %bitcast.1) | data formatting | bytes 1024
Async XLA Ops:
  0.6 1.0 %copy-start = (bf16[128,2048]{1,0:T(8,128)(2,1)S(1)}, bf16[128,2048]{1,0:T(8,128)(2,1)}, u32[]{:S(2)}) copy-start(bf16[128,2048]{1,0:T(8,128)(2,1)} %q_hbm.1) | copy-start | bytes 1572868
  1.7 1.0 %copy-start.1 = (bf16[16,128,128]{2,1,0:T(8,128)(2,1)S(1)}, bf16[16,128,128]{2,1,0:T(8,128)(2,1)}, u32[]{:S(2)}) copy-start(bf16[16,128,128]{2,1,0:T(8,128)(2,1)} %fq_hbm.1) | copy-start | bytes 1572868
  2.7 1.0 %copy-start.2 = (bf16[16,128,128]{2,1,0:T(8,128)(2,1)S(1)}, bf16[16,128,128]{2,1,0:T(8,128)(2,1)}, u32[]{:S(2)}) copy-start(bf16[16,128,128]{2,1,0:T(8,128)(2,1)} %fk_hbm.1) | copy-start | bytes 1572868
  3.8 0.9 %copy-start.3 = (bf16[128,1024]{1,0:T(8,128)(2,1)S(1)}, bf16[128,1024]{1,0:T(8,128)(2,1)}, u32[]{:S(2)}) copy-start(bf16[128,1024]{1,0:T(8,128)(2,1)} %k_hbm.1) | copy-start | bytes 786436
  4.7 0.9 %copy-start.4 = (bf16[128,1024]{1,0:T(8,128)(2,1)S(1)}, bf16[128,1024]{1,0:T(8,128)(2,1)}, u32[]{:S(2)}) copy-start(bf16[128,1024]{1,0:T(8,128)(2,1)} %v_hbm.1) | copy-start | bytes 786436
  5.7 0.7 %copy-start.5 = (s32[12]{0:T(128)S(1)}, s32[12]{0:T(128)}, u32[]{:S(2)}) copy-start(s32[12]{0:T(128)} %dl.1) | copy-start | bytes 148

commit v2 on v1

--- a/solution.py
+++ b/solution.py
@@ -1,4 +1,5 @@
 import functools
+import math
 
 import jax
 import jax.numpy as jnp
@@ -11,7 +12,7 @@
 KVH = 8
 NEG = -1e30
 MESH = pl.DeviceIdType.MESH
-UNROLL = 2
+UNROLL = 4
 
 
 def kernel(
@@ -125,22 +126,28 @@
     load_fq.wait()
     load_fk.wait()
 
-    def prepare(h):
-        p = jnp.dot(qh(h), fq[h], preferred_element_type=jnp.float32)
-        e1 = jnp.exp(p - jnp.max(p, axis=1, keepdims=True))
-        e2 = jnp.exp(jnp.min(p, axis=1, keepdims=True) - p)
-        e1 = e1 / jnp.sum(e1, axis=1, keepdims=True)
-        e2 = e2 / jnp.sum(e2, axis=1, keepdims=True)
-        phiq[h] = jnp.concatenate([e1, e2], axis=1).astype(jnp.bfloat16)
-        fkt[h] = fk[h].T
+    def prepare(hs):
+        ps = [jnp.dot(qh(h), fq[h], preferred_element_type=jnp.float32) for h in hs]
+        turned = [fk[h].T for h in hs]
+        out = []
+        for p in ps:
+            e1 = jnp.exp(p - jnp.max(p, axis=1, keepdims=True))
+            e2 = jnp.exp(jnp.min(p, axis=1, keepdims=True) - p)
+            e1 = e1 * (1.0 / jnp.sum(e1, axis=1, keepdims=True))
+            e2 = e2 * (1.0 / jnp.sum(e2, axis=1, keepdims=True))
+            out.append(jnp.concatenate([e1, e2], axis=1).astype(jnp.bfloat16))
+        for h, t, o in zip(hs, turned, out):
+            fkt[h] = t
+            phiq[h] = o
 
     def heads_loop(lo, hi, fn):
+        U = math.gcd(UNROLL, hi - lo)
+
         def step(t, c):
-            for u in range(UNROLL):
-                fn(lo + t * UNROLL + u)
+            fn([lo + t * U + u for u in range(U)])
             return c
 
-        lax.fori_loop(0, (hi - lo) // UNROLL, step, 0)
+        lax.fori_loop(0, (hi - lo) // U, step, 0)
 
     heads_loop(0, H, prepare)
     sq[...] = jnp.zeros_like(sq)
@@ -158,48 +165,63 @@
         else:
             kpos = anchor - ds[0] * T + jnp.where(kpos >= T, kpos - 2 * T, kpos)
 
-        def one(h):
+        def several(hs):
             mask = kpos >= qstart[:, pl.ds(0, W)]
             if initial:
                 row = anchor + lax.broadcasted_iota(jnp.int32, (T, W), 0)
                 mask = mask & (kpos <= row)
             kth = kt[g, :, pl.ds(0, W)]
-            sc = jnp.dot(qh(h), kth, preferred_element_type=jnp.float32)
-            sc = jnp.where(mask, sc, NEG)
-            top = jnp.max(sc, axis=1, keepdims=True)
+            vxg = vx[g, pl.ds(0, W)]
+            qs = [qh(h) for h in hs]
+            fks = [fkt[h] for h in hs]
+            fqs = [phiq[h] for h in hs]
             if not initial:
-                old = peak[h]
-                new = jnp.maximum(old, top)
-                factor = jnp.exp2((old - new) * c)
-                sub = jnp.concatenate([new, new], axis=1)
+                olds = [peak[h] for h in hs]
+                ats = [acc[h, pl.ds(0, T)] for h in hs]
+                ass = [acc[h, pl.ds(T, T)] for h in hs]
+            results = []
+            for u in range(len(hs)):
+                sc = jnp.dot(qs[u], kth, preferred_element_type=jnp.float32)
+                p = jnp.dot(fks[u], kth, preferred_element_type=jnp.float32)
+                sc = jnp.where(mask, sc, NEG)
+                top = jnp.max(sc, axis=1, keepdims=True)
+                if not initial:
+                    new = jnp.maximum(olds[u], top)
+                    factor = jnp.exp2((olds[u] - new) * c)
+                    sub = jnp.concatenate([new, new], axis=1)
+                else:
+                    new = jnp.broadcast_to(top, (T, D))
+                    sub = new
+                w = jnp.exp2((sc - sub) * c).astype(jnp.bfloat16)
+                e1 = jnp.exp(p - jnp.max(p, axis=0, keepdims=True))
+                e2 = jnp.exp(jnp.min(p, axis=0, keepdims=True) - p)
+                e1 = e1 * (1.0 / jnp.sum(e1, axis=0, keepdims=True))
+                e2 = e2 * (1.0 / jnp.sum(e2, axis=0, keepdims=True))
+                phik = jnp.concatenate([e1, e2], axis=0).astype(jnp.bfloat16)
+                aff = jnp.dot(fqs[u], phik, preferred_element_type=jnp.float32)
+                aff = jnp.where(mask, aff, 0.0).astype(jnp.bfloat16)
+                ot = jnp.dot(w, vxg, preferred_element_type=jnp.float32)
+                os = jnp.dot(aff, vxg, preferred_element_type=jnp.float32)
+                if not initial:
+                    ot = ot + ats[u] * jnp.concatenate([factor, factor], axis=1)
+                    os = os + ass[u]
+                if last:
+                    results.append(ot[:, :D] / ot[:, D:] - os[:, :D] / os[:, D:])
+                else:
+                    results.append((new, ot, os))
+            if last:
+                total = sq[...]
+                for h, r in zip(hs, results):
+                    res[:, pl.ds(pl.multiple_of(h * D, D), D)] = r
+                    total = total + r * r
+                sq[...] = total
             else:
-                new = jnp.broadcast_to(top, (T, D))
-                sub = new
-            w = jnp.exp2((sc - sub) * c).astype(jnp.bfloat16)
-            p = jnp.dot(fkt[h], kth, preferred_element_type=jnp.float32)
-            e1 = jnp.exp(p - jnp.max(p, axis=0, keepdims=True))
-            e2 = jnp.exp(jnp.min(p, axis=0, keepdims=True) - p)
-            e1 = e1 * (1.0 / jnp.sum(e1, axis=0, keepdims=True))
-            e2 = e2 * (1.0 / jnp.sum(e2, axis=0, keepdims=True))
-            phik = jnp.concatenate([e1, e2], axis=0).astype(jnp.bfloat16)
-            aff = jnp.dot(phiq[h], phik, preferred_element_type=jnp.float32)
-            aff = jnp.where(mask, aff, 0.0).astype(jnp.bfloat16)
-            vxg = vx[g, pl.ds(0, W)]
-            ot = jnp.dot(w, vxg, preferred_element_type=jnp.float32)
-            os = jnp.dot(aff, vxg, preferred_element_type=jnp.float32)
-            if not initial:
-                ot = ot + acc[h, pl.ds(0, T)] * jnp.concatenate([factor, factor], axis=1)
-                os = os + acc[h, pl.ds(T, T)]
-            if last:
-                r = ot[:, :D] / ot[:, D:] - os[:, :D] / os[:, D:]
-                res[:, pl.ds(pl.multiple_of(h * D, D), D)] = r
-                sq[...] += r * r
-            else:
-                peak[h] = new
-                acc[h, pl.ds(0, T)] = ot
-                acc[h, pl.ds(T, T)] = os
-
-        heads_loop(g * G, (g + 1) * G, one)
+                for h, (new, ot, os) in zip(hs, results):
+                    peak[h] = new
+                    acc[h, pl.ds(0, T)] = ot
+                    acc[h, pl.ds(T, T)] = os
+
+        heads_loop(g * G, (g + 1) * G, several)
 
     for g in range(KV):
         vx[g, :, pl.ds(D, D)] = jnp.ones((2 * T, D), vx.dtype)
@@ -276,7 +298,7 @@
     KV = max(1, H // (QH // KVH))
     reach = n // 2
     bf, f32 = jnp.bfloat16, jnp.float32
-    hbm = pl.BlockSpec(memory_space=pl.ANY)
+    hbm = pl.BlockSpec(memory_space=pltpu.HBM)
     vm = pl.BlockSpec(memory_space=pltpu.VMEM)
     DMA = pltpu.SemaphoreType.DMA
     res, loss = pl.pallas_call(
@@ -310,7 +332,7 @@
             DMA((nh,)),
         ],
         compiler_params=pltpu.CompilerParams(
-            collective_id=0, has_side_effects=True, vmem_limit_bytes=40 * 1024 * 1024
+            collective_id=0, has_side_effects=True, vmem_limit_bytes=67043328
         ),
     )(doc_lengths, queries, keys, values, fq_weight, fk_weight)
     return res, loss.reshape(T)

time: 42.6 us -> 35.8 us (0.84)
  local copies, waits for them, and re-layouts: 7.15 us -> 2.81 us
  Pallas kernels: 34.5 us -> 32.2 us
    unnamed x14 -> x4, local copies, waits for them, and re-layouts: 7.15 us -> 2.81 us
    pallas_call x1, Pallas kernels: 34.5 us -> 32.2 us  [body(): pl.pallas_call(functools.partial(kernel, n, nh), out_shape=(jax.ShapeDtyp...]
where the time goes in v2:
time: 35.8 us; the launch traced here: 35.7 us
  Pallas kernels  32.2 us (90%)
  local copies, waits for them, and re-layouts  2.81 us (8%)
  between operations  0.65 us (2%)
    pallas_call x1, Pallas kernels, body(): pl.pallas_call(functools.partial(kernel, n, nh), out_shape=(jax.ShapeDtyp...  32.2 us
    unnamed x4, local copies, waits for them, and re-layouts  2.81 us

profile of v2, /device:TPU:0, one launch (start us, length us, event | category | flops | bytes accessed | tf_op | source)
XLA Modules:
  0.0 35.7 jit_solution(8987319904702970709)
XLA Ops:
  0.6 32.2 %shard_map.77 = (f32[128,2048]{1,0:T(8,128)}, f32[1,128]{1,0:T(1,128)}) custom-call(s32[12]{0:T(128)} %dl.1, bf16[128,2048]{1,0:T(8,128)(2,1)} %q_hbm.1, bf16[128,1024]{1,0:T(8,128)(2,1)} %k_hbm.1, bf16[128,1024]{1,0:T(8,128)(2,1)} %v_hbm.1, bf16[16,128,128]{2,1,0:T(8,128)(2,1)} %fq_hbm.1, bf16[16,128,128]{2,1,0:T(8,128)(2,1)} %fk_hbm.1), custom_call_target="tpu_custom_call" | custom-call | tf_op jit(solution)/shard_map/pallas_call | solution.py:304
  32.9 0.0 copy-start
  32.9 2.3 %copy.10 = f32[128,2048]{1,0:T(8,128)} copy(f32[128,2048]{1,0:T(8,128)} %get-tuple-element.8) | data formatting | bytes 2097152
  35.2 0.0 copy-done
  35.2 0.5 %copy.11 = f32[128]{0:T(128)} copy(f32[128]{0:T(128)S(1)} %bitcast.1) | data formatting | bytes 1024
Async XLA Ops:
  32.9 2.3 %copy-start = (f32[1,128]{1,0:T(1,128)S(1)}, f32[1,128]{1,0:T(1,128)}, u32[]{:S(2)}) copy-start(f32[1,128]{1,0:T(1,128)} %get-tuple-element.5) | copy-start | bytes 1540

commit v3 on v1

--- a/solution.py
+++ b/solution.py
@@ -1,4 +1,5 @@
 import functools
+import math
 
 import jax
 import jax.numpy as jnp
@@ -11,12 +12,13 @@
 KVH = 8
 NEG = -1e30
 MESH = pl.DeviceIdType.MESH
-UNROLL = 2
+UNROLL = 4
+LOG2E = 1.4426950408889634
 
 
 def kernel(
     n, nh, dl, q_hbm, k_hbm, v_hbm, fq_hbm, fk_hbm, res, loss,
-    q, fq, fk, fkt, kv, kt, vx, phiq, acc, peak, qstart, sq, lbuf, lrecv,
+    q, fq, fk, fkt, kv, kt, vx, phiq, scores, affin, peak, bias, keep, sq, lbuf, lrecv,
     lsem, osem, ssem, rsem, lssem, lrsem,
 ):
     T = q_hbm.shape[0]
@@ -91,13 +93,19 @@
             device_id=(partner, z), device_id_type=MESH)
 
     anchor = s * T
-    qpos = anchor + lax.broadcasted_iota(jnp.int32, (T, 2 * T), 0)
-    first = jnp.zeros((T, 2 * T), jnp.int32)
+    row = anchor + lax.broadcasted_iota(jnp.int32, (T, T), 0)
+    first = jnp.zeros((T, T), jnp.int32)
     run = jnp.int32(0)
     for i in range(dl.shape[0]):
-        first = jnp.where(qpos >= run, run, first)
+        first = jnp.where(row >= run, run, first)
         run = run + dl[i]
-    qstart[...] = first
+    for d in range(reach + 1):
+        kpos = anchor - d * T + lax.broadcasted_iota(jnp.int32, (T, T), 1)
+        mask = kpos >= first
+        if d == 0:
+            mask = mask & (kpos <= row)
+        bias[:, pl.ds(d * T, T)] = jnp.where(mask, 0.0, NEG)
+        keep[:, pl.ds(d * T, T)] = jnp.where(mask, 1.0, 0.0).astype(jnp.bfloat16)
 
     for d in range(1, reach + 1):
         @pl.when(s < d)
@@ -125,88 +133,95 @@
     load_fq.wait()
     load_fk.wait()
 
-    def prepare(h):
-        p = jnp.dot(qh(h), fq[h], preferred_element_type=jnp.float32)
-        e1 = jnp.exp(p - jnp.max(p, axis=1, keepdims=True))
-        e2 = jnp.exp(jnp.min(p, axis=1, keepdims=True) - p)
-        e1 = e1 / jnp.sum(e1, axis=1, keepdims=True)
-        e2 = e2 / jnp.sum(e2, axis=1, keepdims=True)
-        phiq[h] = jnp.concatenate([e1, e2], axis=1).astype(jnp.bfloat16)
-        fkt[h] = fk[h].T
+    def half(x, axis):
+        top = jnp.max(x, axis=axis, keepdims=True)
+        low = jnp.min(x, axis=axis, keepdims=True)
+        e1 = jnp.exp2(x - top)
+        e2 = jnp.exp2(low - x)
+        e1 = e1 * (1.0 / jnp.sum(e1, axis=axis, keepdims=True))
+        e2 = e2 * (1.0 / jnp.sum(e2, axis=axis, keepdims=True))
+        return jnp.concatenate([e1, e2], axis=axis).astype(jnp.bfloat16)
 
     def heads_loop(lo, hi, fn):
+        U = math.gcd(UNROLL, hi - lo)
+
         def step(t, c):
-            for u in range(UNROLL):
-                fn(lo + t * UNROLL + u)
+            fn([lo + t * U + u for u in range(U)])
             return c
 
-        lax.fori_loop(0, (hi - lo) // UNROLL, step, 0)
-
-    heads_loop(0, H, prepare)
+        lax.fori_loop(0, (hi - lo) // U, step, 0)
+
     sq[...] = jnp.zeros_like(sq)
-    c = (D ** -0.5) * 1.4426950408889634
-
-    def chunk(g, ds, last):
+    c = (D ** -0.5) * LOG2E
+
+    def chunk(g, ds):
         W = T * len(ds)
         initial = ds[0] == 0
+        at = pl.ds(ds[0] * T, W)
         for j, d in enumerate(ds):
             kt[g, :, pl.ds(j * T, T)] = kv[0, g, d].T
-            vx[g, pl.ds(j * T, T), pl.ds(0, D)] = kv[1, g, d]
-        kpos = lax.broadcasted_iota(jnp.int32, (T, W), 1)
-        if initial:
-            kpos = kpos + anchor
-        else:
-            kpos = anchor - ds[0] * T + jnp.where(kpos >= T, kpos - 2 * T, kpos)
-
-        def one(h):
-            mask = kpos >= qstart[:, pl.ds(0, W)]
+            vx[g, pl.ds(d * T, T), pl.ds(0, D)] = kv[1, g, d]
+
+        def several(hs):
+            N = range(len(hs))
+            kth = kt[g, :, pl.ds(0, W)]
+            qs = [qh(h) for h in hs]
             if initial:
-                row = anchor + lax.broadcasted_iota(jnp.int32, (T, W), 0)
-                mask = mask & (kpos <= row)
-            kth = kt[g, :, pl.ds(0, W)]
-            sc = jnp.dot(qh(h), kth, preferred_element_type=jnp.float32)
-            sc = jnp.where(mask, sc, NEG)
-            top = jnp.max(sc, axis=1, keepdims=True)
-            if not initial:
-                old = peak[h]
-                new = jnp.maximum(old, top)
-                factor = jnp.exp2((old - new) * c)
-                sub = jnp.concatenate([new, new], axis=1)
+                fks = [fk[h].T for h in hs]
+                pq = [jnp.dot(qs[u], fq[hs[u]], preferred_element_type=jnp.float32) for u in N]
             else:
-                new = jnp.broadcast_to(top, (T, D))
-                sub = new
-            w = jnp.exp2((sc - sub) * c).astype(jnp.bfloat16)
-            p = jnp.dot(fkt[h], kth, preferred_element_type=jnp.float32)
-            e1 = jnp.exp(p - jnp.max(p, axis=0, keepdims=True))
-            e2 = jnp.exp(jnp.min(p, axis=0, keepdims=True) - p)
-            e1 = e1 * (1.0 / jnp.sum(e1, axis=0, keepdims=True))
-            e2 = e2 * (1.0 / jnp.sum(e2, axis=0, keepdims=True))
-            phik = jnp.concatenate([e1, e2], axis=0).astype(jnp.bfloat16)
-            aff = jnp.dot(phiq[h], phik, preferred_element_type=jnp.float32)
-            aff = jnp.where(mask, aff, 0.0).astype(jnp.bfloat16)
-            vxg = vx[g, pl.ds(0, W)]
-            ot = jnp.dot(w, vxg, preferred_element_type=jnp.float32)
-            os = jnp.dot(aff, vxg, preferred_element_type=jnp.float32)
-            if not initial:
-                ot = ot + acc[h, pl.ds(0, T)] * jnp.concatenate([factor, factor], axis=1)
-                os = os + acc[h, pl.ds(T, T)]
-            if last:
-                r = ot[:, :D] / ot[:, D:] - os[:, :D] / os[:, D:]
+                fks = [fkt[h] for h in hs]
+                fqs = [phiq[h] for h in hs]
+                tops = [peak[h] for h in hs]
+            both = jnp.dot(jnp.concatenate(fks + qs, axis=0), kth, preferred_element_type=jnp.float32)
+            if initial:
+                fqs = [half(p * LOG2E, 1) for p in pq]
+            phiks = [half(both[u * F:(u + 1) * F] * LOG2E, 0) for u in N]
+            affs = [jnp.dot(fqs[u], phiks[u], preferred_element_type=jnp.float32) for u in N]
+            both = both[len(hs) * F:]
+            scs = [both[u * T:(u + 1) * T] + bias[:, at] for u in N]
+            news = []
+            for u in N:
+                new = scs[u][:, :T]
+                for j in range(1, len(ds)):
+                    new = jnp.maximum(new, scs[u][:, j * T:(j + 1) * T])
+                news.append(new if initial else jnp.maximum(new, tops[u]))
+            affs = [x.astype(jnp.bfloat16) * keep[:, at] for x in affs]
+            for u, h in enumerate(hs):
+                if initial:
+                    fkt[h] = fks[u]
+                    phiq[h] = fqs[u]
+                peak[h] = news[u]
+                scores[h, :, at] = scs[u]
+                affin[h, :, at] = affs[u]
+
+        heads_loop(g * G, (g + 1) * G, several)
+
+    def finish(g):
+        def several(hs):
+            N = range(len(hs))
+            vxg = vx[g]
+            tops = [jnp.max(peak[h], axis=1, keepdims=True) for h in hs]
+            ws = [jnp.exp2((scores[hs[u]] - tops[u]) * c).astype(jnp.bfloat16) for u in N]
+            affs = [affin[h] for h in hs]
+            both = jnp.dot(jnp.concatenate(ws + affs, axis=0), vxg, preferred_element_type=jnp.float32)
+            ots = [both[u * T:(u + 1) * T] for u in N]
+            oss = [both[(len(hs) + u) * T:(len(hs) + u + 1) * T] for u in N]
+            results = [ots[u][:, :D] / ots[u][:, D:] - oss[u][:, :D] / oss[u][:, D:] for u in N]
+            total = sq[...]
+            for h, r in zip(hs, results):
                 res[:, pl.ds(pl.multiple_of(h * D, D), D)] = r
-                sq[...] += r * r
-            else:
-                peak[h] = new
-                acc[h, pl.ds(0, T)] = ot
-                acc[h, pl.ds(T, T)] = os
-
-        heads_loop(g * G, (g + 1) * G, one)
+                total = total + r * r
+            sq[...] = total
+
+        heads_loop(g * G, (g + 1) * G, several)
 
     for g in range(KV):
-        vx[g, :, pl.ds(D, D)] = jnp.ones((2 * T, D), vx.dtype)
+        vx[g, :, pl.ds(D, D)] = jnp.ones(((reach + 1) * T, D), vx.dtype)
     for g in range(KV):
         for i in range(2):
             own_loads[i][g].wait()
-        chunk(g, (0,), False)
+        chunk(g, (0,))
 
     def pass_on(g, e):
         @pl.when(s >= 2 * e)
@@ -229,7 +244,9 @@
             def _():
                 for i in range(2):
                     arrived(i, g, 2 * e - 1).wait_recv()
-            chunk(g, (2 * e - 1, 2 * e), e == E)
+            chunk(g, (2 * e - 1, 2 * e))
+            if e == E:
+                finish(g)
 
     part = jnp.sum(sq[...].T, axis=0, keepdims=True) * (1.0 / D)
     lbuf[...] = jnp.broadcast_to(part, lbuf.shape)
@@ -276,7 +293,7 @@
     KV = max(1, H // (QH // KVH))
     reach = n // 2
     bf, f32 = jnp.bfloat16, jnp.float32
-    hbm = pl.BlockSpec(memory_space=pl.ANY)
+    hbm = pl.BlockSpec(memory_space=pltpu.HBM)
     vm = pl.BlockSpec(memory_space=pltpu.VMEM)
     DMA = pltpu.SemaphoreType.DMA
     res, loss = pl.pallas_call(
@@ -294,11 +311,13 @@
             pltpu.VMEM((H, F, D), bf),
             pltpu.VMEM((2, KV, reach + 1, T, D), bf),
             pltpu.VMEM((KV, D, 2 * T), bf),
-            pltpu.VMEM((KV, 2 * T, 2 * D), bf),
+            pltpu.VMEM((KV, (reach + 1) * T, 2 * D), bf),
             pltpu.VMEM((H, T, 2 * F), bf),
-            pltpu.VMEM((H, 2 * T, 2 * D), f32),
+            pltpu.VMEM((H, T, (reach + 1) * T), f32),
+            pltpu.VMEM((H, T, (reach + 1) * T), bf),
             pltpu.VMEM((H, T, D), f32),
-            pltpu.VMEM((T, 2 * T), jnp.int32),
+            pltpu.VMEM((T, (reach + 1) * T), f32),
+            pltpu.VMEM((T, (reach + 1) * T), bf),
             pltpu.VMEM((T, D), f32),
             pltpu.VMEM((8, T), f32),
             pltpu.VMEM((nh, 8, T), f32),
@@ -310,7 +329,7 @@
             DMA((nh,)),
         ],
         compiler_params=pltpu.CompilerParams(
-            collective_id=0, has_side_effects=True, vmem_limit_bytes=40 * 1024 * 1024
+            collective_id=0, has_side_effects=True, vmem_limit_bytes=67043328
         ),
     )(doc_lengths, queries, keys, values, fq_weight, fk_weight)
     return res, loss.reshape(T)

time: 42.6 us -> 26.1 us (0.61)
  the two profiles are of different devices: /device:TPU:0 before, /device:TPU:4 now
where the time goes in v3:
time: 26.1 us; the launch traced here: 25.9 us
  Pallas kernels  22.5 us (86%)
  local copies, waits for them, and re-layouts  2.81 us (11%)
  between operations  0.65 us (2%)
    pallas_call x1, Pallas kernels, body(): pl.pallas_call(functools.partial(kernel, n, nh), out_shape=(jax.ShapeDtyp...  22.5 us
    unnamed x4, local copies, waits for them, and re-layouts  2.81 us

profile of v3, /device:TPU:4, one launch (start us, length us, event | category | flops | bytes accessed | tf_op | source)
XLA Modules:
  0.0 25.9 jit_solution(14794912650620660881)
XLA Ops:
  0.6 22.5 %shard_map.77 = (f32[128,2048]{1,0:T(8,128)}, f32[1,128]{1,0:T(1,128)}) custom-call(s32[12]{0:T(128)} %dl.1, bf16[128,2048]{1,0:T(8,128)(2,1)} %q_hbm.1, bf16[128,1024]{1,0:T(8,128)(2,1)} %k_hbm.1, bf16[128,1024]{1,0:T(8,128)(2,1)} %v_hbm.1, bf16[16,128,128]{2,1,0:T(8,128)(2,1)} %fq_hbm.1, bf16[16,128,128]{2,1,0:T(8,128)(2,1)} %fk_hbm.1), custom_call_target="tpu_custom_call" | custom-call | tf_op jit(solution)/shard_map/pallas_call | solution.py:299
  23.1 0.0 copy-start
  23.1 2.3 %copy.10 = f32[128,2048]{1,0:T(8,128)} copy(f32[128,2048]{1,0:T(8,128)} %get-tuple-element.8) | data formatting | bytes 2097152
  25.4 0.0 copy-done
  25.4 0.5 %copy.11 = f32[128]{0:T(128)} copy(f32[128]{0:T(128)S(1)} %bitcast.1) | data formatting | bytes 1024
Async XLA Ops:
  23.1 2.3 %copy-start = (f32[1,128]{1,0:T(1,128)S(1)}, f32[1,128]{1,0:T(1,128)}, u32[]{:S(2)}) copy-start(f32[1,128]{1,0:T(1,128)} %get-tuple-element.5) | copy-start | bytes 1540
